TPU v7x, 128 devices: a whole 4x4x4 slice. The times are simulated.
128 devices in a mesh: front: 4 (over x), row: 4 (over y), col: 8 (over z, core).
Axes of the slice: x: 4, y: 4, z: 4, core: 2. Of those that a mesh axis runs over, the one named last changes fastest.
Arguments:
- front_in: float32 [32768, 8192], P(('front', 'row'), 'col'), parts along dimension 0, may hold values from -6 to 6
- child_tiles: bfloat16 [128, 224, 128, 128], P(('front', 'row', 'col')), parts along dimension 0, may hold values from -6 to 6
- child_map: int32 [128, 224], P(('front', 'row', 'col')), parts along dimension 0, may hold values from 0 to 4095, as said below
- pattern: int32 [256, 64], P('front'), parts along dimension 0, may hold values 0 or 1
- pivot_inverse: float32 [8, 512, 512], P('front'), parts along dimension 0, may hold values from -0.01171875 to 0.01171875
Outputs:
- front_out: float32 [32768, 8192], P(('front', 'row'), 'col'), parts along dimension 0
There are 4 independent parts, one for each index of `front`. A program takes and returns all parts, laid end to end along the dimension named above; each array names one. Nothing has to cross between parts.
Inputs may be any that keep to these rules, and one draw needn't show every extreme that they name: Entries j * 7 to (j + 1) * 7 - 1 of each row of child_map name tiles held by device j of the front's grid, j = grid row * 8 + grid column, that device holding tile rows of its 2048 rows and tile columns of its 1024 columns.
All inputs are finite; a program needn't handle non-finite values.
Results may differ from a plain program's by a relative error of at most 0.0062.
Values may be sent and summed in bfloat16 or wider, within the bound.
A program may use at most 128 MiB of HBM per device.

v0:
```python
import jax
import jax.numpy as jnp
from jax import lax
from jax.sharding import Mesh
from jax.sharding import PartitionSpec as P

TILE = 128
PANEL = 512
PANELS = 2
SLOTS = 7
NT = 64
COL = ("col_0", "col_1")
ROW_COL = ("row", "col_0", "col_1")
FRONT_ROW_COL = ("front", "row", "col_0", "col_1")


def from_root(x, axes, root):
    x = jnp.where(lax.axis_index(axes) == root, x, jnp.zeros_like(x))
    for axis in axes:
        x = lax.psum(x, axis)
    return x


def cut_along(x, dim, count):
    shape = x.shape
    pieces = x.reshape(*shape[:dim], count, shape[dim] // count, *shape[dim + 1 :])
    return jnp.moveaxis(pieces, dim, 0)


def edges_of(length, count):
    lap = length // count
    if lap >= 8:
        lap -= lap % 8
    return [lap * k for k in range(1, count)]


def laid_out(pieces, dim):
    pieces = jnp.moveaxis(pieces, 0, dim)
    shape = pieces.shape
    return pieces.reshape(*shape[:dim], shape[dim] * shape[dim + 1], *shape[dim + 2 :])


def cut_exchange(x, axis, pieces, split_dim, concat_dim):
    blocks = cut_along(x, split_dim, lax.axis_size(axis))
    cut = max(range(1, max(2, blocks.ndim - 1)), key=lambda d: blocks.shape[d])
    gathered = []
    for piece in jnp.split(blocks, edges_of(blocks.shape[cut], pieces), axis=cut):
        if piece.size:
            gathered.append(lax.all_to_all(piece, axis, split_axis=0, concat_axis=0, tiled=True))
    return laid_out(jnp.concatenate(gathered, axis=cut), concat_dim)


def padded_to(lines, count):
    spare = -lines.shape[0] % count
    if not spare:
        return lines
    return jnp.concatenate([lines, jnp.zeros((spare, *lines.shape[1:]), lines.dtype)])


def spread(x, axis, root):
    lines = jnp.where(lax.axis_index(axis) == root, x, jnp.zeros_like(x)).reshape(
        -1, *x.shape[1:][-1:]
    )
    padded = padded_to(lines, lax.axis_size(axis))
    own = lax.psum_scatter(padded, axis, scatter_dimension=0, tiled=True)
    return lax.all_gather(own, axis, axis=0, tiled=True)[: len(lines)].reshape(x.shape)


def factor_panel(matrix, inverse, panel_index):
    first_col = panel_index * PANEL
    lower_part = jnp.dot(
        matrix[:, first_col : first_col + PANEL],
        inverse[panel_index],
        precision=lax.Precision.HIGHEST,
        preferred_element_type=jnp.float32,
    )
    shared = from_root(lower_part.astype(jnp.bfloat16), COL, 0)
    return (lower_part, shared)


def apply_update(
    matrix, shared, upper_rows, finish, first_col, last_col, row_global, col_global, tile_mask
):
    if last_col <= first_col:
        return matrix
    row_count = matrix.shape[0]
    product = jnp.dot(shared, upper_rows[:, first_col:last_col], preferred_element_type=jnp.float32)
    width = last_col - first_col
    pattern_part = tile_mask[:, first_col // TILE : last_col // TILE]
    product = (
        product.reshape(row_count // TILE, TILE, width // TILE, TILE)
        * pattern_part[:, None, :, None]
    ).reshape(row_count, width)
    active_mask = (row_global >= finish)[:, None] & (col_global[first_col:last_col] >= finish)[
        None, :
    ]
    return matrix.at[:, first_col:last_col].add(-jnp.where(active_mask, product, 0.0))


def body(front_in, child_tiles, child_map, pattern, pivot_inverse):
    row_count, col_count = front_in.shape
    grid_rows = lax.axis_size("row")
    grid_cols = lax.axis_size(COL)
    groups = grid_rows * grid_cols
    row_index = lax.axis_index("row")
    col_index = lax.axis_index(COL)
    tile_rows = row_count // TILE
    tile_cols = col_count // TILE
    outgoing = child_tiles.reshape(grid_rows, grid_cols, SLOTS, TILE, TILE)
    targets = child_map.reshape(grid_rows, grid_cols, SLOTS)
    arrived, placed = (
        cut_exchange(outgoing.reshape(groups, SLOTS, TILE, TILE), ROW_COL, 2, 0, 0),
        cut_exchange(targets.reshape(groups, SLOTS), ROW_COL, 2, 0, 0),
    )
    child_flat = arrived.reshape(-1, TILE, TILE).astype(jnp.float32)
    flat_targets = placed.reshape(-1)
    local_row = flat_targets // NT - row_index * tile_rows
    local_col = flat_targets % NT - col_index * tile_cols
    matrix = (
        front_in.reshape(tile_rows, TILE, tile_cols, TILE)
        .at[local_row, :, local_col, :]
        .add(child_flat)
        .reshape(row_count, col_count)
    )
    row_global = row_index * row_count + jnp.arange(row_count)
    col_global = col_index * col_count + jnp.arange(col_count)
    tile_mask = lax.dynamic_slice(
        pattern, (row_index * tile_rows, col_index * tile_cols), (tile_rows, tile_cols)
    ).astype(jnp.float32)
    lower_part, shared = factor_panel(matrix, pivot_inverse, 0)
    for panel_index in range(PANELS):
        first_col = panel_index * PANEL
        finish = first_col + PANEL
        upper_rows = spread(matrix[first_col:finish, :].astype(jnp.bfloat16), "row", 0)
        stored = (row_global >= finish)[:, None] & (col_index == 0)
        matrix = matrix.at[:, first_col:finish].set(
            jnp.where(stored, lower_part, matrix[:, first_col:finish])
        )
        if panel_index + 1 < PANELS:
            matrix = apply_update(
                matrix,
                shared,
                upper_rows,
                finish,
                finish,
                finish + PANEL,
                row_global,
                col_global,
                tile_mask,
            )
            following = factor_panel(matrix, pivot_inverse, panel_index + 1)
            matrix = apply_update(
                matrix, shared, upper_rows, finish, 0, finish, row_global, col_global, tile_mask
            )
            matrix = apply_update(
                matrix,
                shared,
                upper_rows,
                finish,
                finish + PANEL,
                col_count,
                row_global,
                col_global,
                tile_mask,
            )
        else:
            matrix = apply_update(
                matrix, shared, upper_rows, finish, 0, col_count, row_global, col_global, tile_mask
            )
            following = (lower_part, shared)
        lower_part, shared = following
    return matrix


def solution(mesh):
    torus = Mesh(
        mesh.devices.reshape(mesh.shape["front"], mesh.shape["row"], 4, 2),
        ("front", "row", "col_0", "col_1"),
    )
    placed = (
        P(("front", "row"), COL),
        P(FRONT_ROW_COL, None, None, None),
        P(FRONT_ROW_COL, None),
        P("front", None),
        P("front", None, None),
    )
    return jax.shard_map(
        body, mesh=torus, in_specs=placed, out_specs=P(("front", "row"), COL), check_vma=False
    )
```

profile of v0, /device:TPU:1, one launch (start us, length us, event | category | flops | bytes accessed | tf_op | source)
XLA Modules:
  0.0 445.0 jit_solution(7594469492940474296)
XLA Ops:
  10.0 9.6 %all-to-all-start = ((s32[32,1,7]{2,1,0:T(1,128)}), s32[32,1,7]{2,1,0:T(1,128)S(1)}, u32[]{:S(2)}, u32[]{:S(2)}) async-start(s32[32,1,7]{2,1,0:T(1,128)} %bitcast), calls=%async_computation | async-start | bytes 32768 | tf_op jit(solution)/shard_map/all_to_all | solution.py:49
  19.6 8.1 %fusion.26 = (bf16[32,1,7,64,128]{4,3,2,1,0:T(8,128)(2,1)}, bf16[32,1,7,64,128]{4,3,2,1,0:T(8,128)(2,1)}) fusion(bf16[32,1,7,128,128]{4,3,2,1,0:T(8,128)(2,1)} %bitcast.72), kind=kLoop, calls=%fused_computation.61 | loop fusion | bytes 14680064 | tf_op jit(solution)/shard_map/split | solution.py:47
  27.7 52.8 %all_to_all.15 = bf16[32,1,7,64,128]{4,3,2,1,0:T(8,128)(2,1)} all-to-all(bf16[32,1,7,64,128]{4,3,2,1,0:T(8,128)(2,1)} %get-tuple-element.73), channel_id=1, replica_groups=mesh['front'=4,'row'=4,'col_0'=4,'col_1'=2] {'row','col_0','col_1'}, dimensions={0} | all-to-all | bytes 7340032 | tf_op jit(solution)/shard_map/all_to_all | solution.py:49
  80.5 4.6 %all-to-all-start.2 = ((bf16[32,1,7,64,128]{4,3,2,1,0:T(8,128)(2,1)}), bf16[32,1,7,64,128]{4,3,2,1,0:T(8,128)(2,1)}, u32[]{:S(2)}, u32[]{:S(2)}) async-start(bf16[32,1,7,64,128]{4,3,2,1,0:T(8,128)(2,1)} %get-tuple-element.74), calls=%async_computation.2 | async-start | bytes 7340032 | tf_op jit(solution)/shard_map/all_to_all | solution.py:49
  85.4 5.5 %copy.14 = f32[256,8,8,128]{3,2,1,0:T(8,128)S(1)} copy(f32[256,8,8,128]{3,1,2,0:T(8,128)} %bitcast.71) | data formatting | bytes 16777216
  90.8 4.9 %copy.11 = f32[16,128,8,128]{3,1,2,0:T(8,128)} copy(f32[16,128,8,128]{3,2,1,0:T(8,128)S(1)} %bitcast.68) | data formatting | bytes 16777216 | tf_op jit(solution)/shard_map/reshape | solution.py:120
  96.5 34.4 %all-to-all-done.2 = bf16[32,1,7,64,128]{4,3,2,1,0:T(8,128)(2,1)} async-done(((bf16[32,1,7,64,128]{4,3,2,1,0:T(8,128)(2,1)}), bf16[32,1,7,64,128]{4,3,2,1,0:T(8,128)(2,1)}, u32[]{:S(2)}, u32[]{:S(2)}) %all-to-all-start.2) | async-done | bytes 3670048 | tf_op jit(solution)/shard_map/all_to_all | solution.py:49
  130.9 8.9 %pad_maximum_fusion = bf16[32,1,7,128,128]{4,3,2,1,0:T(8,128)(2,1)} fusion(bf16[32,1,7,64,128]{4,3,2,1,0:T(8,128)(2,1)} %all-to-all-done.2, bf16[32,1,7,64,128]{4,3,2,1,0:T(8,128)(2,1)} %all_to_all.15), kind=kLoop, calls=%fused_computation.6 | loop fusion | flops 14680064 | bytes 14680064 | tf_op jit(solution)/shard_map/concatenate | solution.py:50
  139.7 10.1 %bitcast_convert_fusion = f32[224,128,128]{2,1,0:T(8,128)} fusion(bf16[32,1,7,128,128]{4,3,2,1,0:T(8,128)(2,1)} %pad_maximum_fusion), kind=kLoop, calls=%fused_computation.7 | loop fusion | flops 3670016 | bytes 22020096 | tf_op jit(solution)/shard_map/convert_element_type | solution.py:115
  149.8 46.9 %scatter_fusion = f32[16,128,8,128]{3,1,2,0:T(8,128)} fusion(f32[16,128,8,128]{3,1,2,0:T(8,128)} %copy.11, s32[224]{0:T(256)S(1)} %bitcast.70, f32[224,128,128]{2,1,0:T(8,128)} %bitcast_convert_fusion), kind=kCustom, calls=%fused_computation | custom fusion | flops 3670016 | bytes 44041984 | tf_op jit(solution)/shard_map/scatter-add | solution.py:122
  200.8 9.9 %copy.12 = f32[16,128,8,128]{3,2,1,0:T(8,128)S(1)} copy(f32[16,128,8,128]{3,1,2,0:T(8,128)} %scatter_fusion) | data formatting | bytes 16777216 | tf_op jit(solution)/shard_map/scatter-add | solution.py:122
  212.9 8.9 %convert_select_fusion.1 = (bf16[2048,512]{1,0:T(8,128)(2,1)}, f32[2048,512]{1,0:T(8,128)}) fusion(pred[]{:T(512)S(6)} %eq.6, f32[2,512,512]{2,1,0:T(8,128)S(1)} %copy-done.2, f32[2048,1024]{1,0:T(8,128)S(1)} %bitcast.64), kind=kOutput, calls=%fused_computation.26 | convolution fusion | flops 6444548096 | bytes 11534337 | tf_op jit(solution)/shard_map/dot_general | solution.py:71
  223.3 57.6 %all-reduce.5.cloned.1.call-done = bf16[2048,512]{1,0:T(8,128)(2,1)} async-done(((bf16[2048,512]{1,0:T(8,128)(2,1)}), bf16[2048,512]{1,0:T(8,128)(2,1)}) %all-reduce.5.cloned.1.call-update) | async-done | bytes 2097168 | tf_op jit(solution)/shard_map/psum | solution.py:20
  282.6 5.8 %fusion.3 = f32[2048,1024]{1,0:T(8,128)} fusion(f32[2048,1024]{1,0:T(8,128)} %bitcast.65, f32[2048,512]{1,0:T(8,128)} %get-tuple-element.80, pred[2048]{0:T(1024)(128)(4,1)S(1)} %get-tuple-element.86, pred[]{:T(512)} %compare_reduce_fusion), kind=kLoop, calls=%fused_computation.10 | loop fusion | flops 2097152 | bytes 12585472 | tf_op jit(solution)/shard_map/scatter | solution.py:136
  288.4 21.7 %all-reduce.7.cloned.1.call-done = bf16[2048,512]{1,0:T(8,128)(2,1)} async-done(((bf16[2048,512]{1,0:T(8,128)(2,1)}), bf16[2048,512]{1,0:T(8,128)(2,1)}) %all-reduce.7.cloned.1.call-update) | async-done | bytes 2097168 | tf_op jit(solution)/shard_map/psum | solution.py:20
  311.6 5.9 %constant_dynamic-update-slice_fusion = (f32[2048,1024]{1,0:T(8,128)}, f32[2048,512]{1,0:T(8,128)}) fusion(f32[2048,1024]{1,0:T(8,128)} %fusion.3, f32[256,8,4,128]{3,2,1,0:T(4,128)S(1)} %bitcast.69, bf16[2048,512]{1,0:T(8,128)(2,1)S(1)} %copy-done.3, bf16[512,1024]{1,0:T(8,128)(2,1)S(1)} %copy-done.4, pred[512]{0:T(512)(128)(4,1)S(1)} %get-tuple-element.78, ...), kind=kOutput, calls=%fused_computation.60 | convolution fusion | flops 1078984704 | bytes 19401216 | tf_op jit(solution)/shard_map/dot_general | solution.py:87
  318.1 5.5 %fusion.4 = f32[2048,1024]{1,0:T(8,128)} fusion(f32[2048,1024]{1,0:T(8,128)} %get-tuple-element.81, f32[256,8,4,128]{3,2,1,0:T(4,128)S(1)} %bitcast.73, bf16[2048,512]{1,0:T(8,128)(2,1)S(1)} %copy-done.3, pred[512]{0:T(512)(128)(4,1)S(1)} %get-tuple-element.77, pred[]{:T(512)} %compare_reduce_fusion, pred[2048]{0:T(1024)(128)(4,1)S(1)} %get-tuple-element.85, ...), kind=kOutput, calls=%fused_computation.11 | convolution fusion | flops 1080033280 | bytes 15207424 | tf_op jit(solution)/shard_map/dot_general | solution.py:87
  323.6 2.7 fusion.14
  326.4 10.4 %fusion.10 = (f32[2048,1024]{1,0:T(8,128)}, bf16[2048,512]{1,0:T(8,128)(2,1)S(1)}) fusion(f32[2048,1024]{1,0:T(8,128)} %fusion.4, pred[2048]{0:T(1024)(128)(4,1)S(1)} %broadcast_and_fusion, f32[2048,512]{1,0:T(8,128)} %get-tuple-element.82, f32[2,512,512]{2,1,0:T(8,128)S(1)} %copy-done.2), kind=kOutput, calls=%fused_computation.20 | convolution fusion | flops 6444548096 | bytes 15730688 | tf_op jit(solution)/shard_map/dot_general | solution.py:71
  338.4 11.2 %reduce-scatter.5.cloned.1.call-done = bf16[128,1024]{1,0:T(8,128)(2,1)} async-done(((bf16[512,1024]{1,0:T(8,128)(2,1)}), bf16[128,1024]{1,0:T(8,128)(2,1)}) %reduce-scatter.5.cloned.1.call-update) | async-done | bytes 262160 | tf_op jit(solution)/shard_map/reduce_scatter | solution.py:65
  349.7 48.4 %all-reduce.9.cloned.1.call-done = bf16[2048,512]{1,0:T(8,128)(2,1)} async-done(((bf16[2048,512]{1,0:T(8,128)(2,1)}), bf16[2048,512]{1,0:T(8,128)(2,1)}) %all-reduce.9.cloned.1.call-update) | async-done | bytes 2097168 | tf_op jit(solution)/shard_map/psum | solution.py:20
  398.1 29.0 %all-reduce.11.cloned.1.call-done = bf16[2048,512]{1,0:T(8,128)(2,1)} async-done(((bf16[2048,512]{1,0:T(8,128)(2,1)}), bf16[2048,512]{1,0:T(8,128)(2,1)}) %all-reduce.11.cloned.1.call-update) | async-done | bytes 2097168 | tf_op jit(solution)/shard_map/psum | solution.py:20
  427.7 2.8 copy-done.1
  430.5 7.2 %fusion.2 = f32[2048,1024]{1,0:T(8,128)} fusion(f32[2048,1024]{1,0:T(8,128)S(1)} %copy-done.1, f32[256,8,8,128]{3,2,1,0:T(8,128)S(1)} %bitcast.66, bf16[2048,512]{1,0:T(8,128)(2,1)} %all-reduce.11.cloned.1.call-done, bf16[512,1024]{1,0:T(8,128)(2,1)} %all-gather.5.cloned.1.call-done, pred[1024]{0:T(1024)(128)(4,1)S(1)} %broadcast_compare_fusion, ...), kind=kOutput, calls=%fused_computation.4 | convolution fusion | flops 2157969408 | bytes 28314624 | tf_op jit(solution)/shard_map/dot_general | solution.py:87
  (52 shorter events, 17.4 us)
Async XLA Ops:
  10.0 17.7 %all-to-all-start = ((s32[32,1,7]{2,1,0:T(1,128)}), s32[32,1,7]{2,1,0:T(1,128)S(1)}, u32[]{:S(2)}, u32[]{:S(2)}) async-start(s32[32,1,7]{2,1,0:T(1,128)} %bitcast), calls=%async_computation | async-start | bytes 32768 | tf_op jit(solution)/shard_map/all_to_all | solution.py:49
  80.5 50.4 %all-to-all-start.2 = ((bf16[32,1,7,64,128]{4,3,2,1,0:T(8,128)(2,1)}), bf16[32,1,7,64,128]{4,3,2,1,0:T(8,128)(2,1)}, u32[]{:S(2)}, u32[]{:S(2)}) async-start(bf16[32,1,7,64,128]{4,3,2,1,0:T(8,128)(2,1)} %get-tuple-element.74), calls=%async_computation.2 | async-start | bytes 7340032 | tf_op jit(solution)/shard_map/all_to_all | solution.py:49
  85.1 138.1 %reduce-scatter.3.cloned.1.call-start = ((), (), s32[]{:S(2)}) async-start(), calls=%async_computation.7 | async-start | bytes 1310720 | tf_op jit(solution)/shard_map/reduce_scatter | solution.py:65
  200.5 80.4 %all-reduce.5.cloned.1.call-start = ((), (), s32[]{:S(2)}) async-start(), calls=%async_computation.5 | async-start | bytes 4194304 | tf_op jit(solution)/shard_map/psum | solution.py:20
  210.7 2.2 copy-start.2
  212.9 8.9 %copy-start = (f32[256,8,8,128]{3,1,2,0:T(8,128)}, f32[256,8,8,128]{3,1,2,0:T(8,128)S(1)}, u32[]{:S(2)}) copy-start(f32[256,8,8,128]{3,1,2,0:T(8,128)S(1)} %copy.25) | copy-start | bytes 25165828
  221.8 66.6 %all-gather.3.cloned.1.call-start = ((), (), s32[]{:S(2)}) async-start(), calls=%async_computation.8 | async-start | bytes 1310720 | tf_op jit(solution)/shard_map/all_gather | solution.py:66
  223.3 86.8 %all-reduce.7.cloned.1.call-start = ((), (), s32[]{:S(2)}) async-start(), calls=%async_computation.6 | async-start | bytes 4194304 | tf_op jit(solution)/shard_map/psum | solution.py:20
  281.0 68.6 %reduce-scatter.5.cloned.1.call-start = ((), (), s32[]{:S(2)}) async-start(), calls=%async_computation.11 | async-start | bytes 1310720 | tf_op jit(solution)/shard_map/reduce_scatter | solution.py:65
  288.4 22.3 %copy-start.4 = (bf16[512,1024]{1,0:T(8,128)(2,1)S(1)}, bf16[512,1024]{1,0:T(8,128)(2,1)}, u32[]{:S(2)}) copy-start(bf16[512,1024]{1,0:T(8,128)(2,1)} %all-gather.3.cloned.1.call-done) | copy-start | bytes 3145732
  310.0 1.6 copy-start.3
  326.3 71.7 %all-reduce.9.cloned.1.call-start = ((), (), s32[]{:S(2)}) async-start(), calls=%async_computation.9 | async-start | bytes 4194304 | tf_op jit(solution)/shard_map/psum | solution.py:20
  338.3 59.8 %all-gather.5.cloned.1.call-start = ((), (), s32[]{:S(2)}) async-start(), calls=%async_computation.12 | async-start | bytes 1310720 | tf_op jit(solution)/shard_map/all_gather | solution.py:66
  349.6 77.5 %all-reduce.11.cloned.1.call-start = ((), (), s32[]{:S(2)}) async-start(), calls=%async_computation.10 | async-start | bytes 4194304 | tf_op jit(solution)/shard_map/psum | solution.py:20
  427.1 3.4 copy-start.1
Sparse Core Ops, SparseCore 0:
  200.6 22.5 reduce-scatter.2
  225.0 24.1 all-gather.2
  326.4 23.0 reduce-scatter.4
  351.1 24.1 all-gather.4
Sparse Core Ops, SparseCore 1:
  221.9 59.0 all-reduce.4
  283.4 26.6 all-reduce.6
  338.4 59.6 all-reduce.8
  400.5 26.6 all-reduce.10
where the time goes:
time: 446 us; the launch traced here: 445 us
  waiting for transfers between devices  204 us (46%)
  other arithmetic  81 us (18%)
  blocking collectives  52.8 us (12%)
  local copies, waits for them, and re-layouts  39.5 us (9%)
  matrix products  37.9 us (8%)
  starting transfers between devices  15 us (3%)
  between operations  15 us (3%)
    psum x4, waiting for transfers between devices, from_root(): x = lax.psum(x, axis)  157 us
    all_to_all x1, blocking collectives, cut_exchange(): lax.all_to_all(piece, axis, split_axis=0, concat_axis=0, tiled=True)  52.8 us
    scatter-add x1, other arithmetic, body(): matrix = front_in.reshape(tile_rows, TILE, tile_cols, TILE).at[local_row,...  46.9 us
    all_to_all x2, waiting for transfers between devices, cut_exchange(): lax.all_to_all(piece, axis, split_axis=0, concat_axis=0, tiled=True)  34.4 us
    dot_general x2, matrix products, factor_panel(): jnp.dot(matrix[:, first_col:first_col + PANEL], inverse[panel_index], pre...  19.3 us
    dot_general x3, matrix products, apply_update(): jnp.dot(shared, upper_rows[:, first_col:last_col], preferred_element_type...  18.6 us
    all_to_all x2, starting transfers between devices, cut_exchange(): lax.all_to_all(piece, axis, split_axis=0, concat_axis=0, tiled=True)  14.2 us
    unnamed x14, local copies, waits for them, and re-layouts  13.2 us
  transfers between devices with their start and end apart: 10, of which 7 were waited for; matrix products, arithmetic and copies ran while one was open for 13% of the time, Pallas kernels for 0%

commit v1 on v0

--- a/solution.py
+++ b/solution.py
@@ -17,7 +17,7 @@
 def from_root(x, axes, root):
     x = jnp.where(lax.axis_index(axes) == root, x, jnp.zeros_like(x))
     for axis in axes:
-        x = lax.psum(x, axis)
+        x = jnp.sum(lax.all_gather(x, axis), axis=0)
     return x
 
 

time: 446 us -> 551 us (1.24)
  waiting for transfers between devices: 204 us -> 259 us
  other arithmetic: 81 us -> 110 us
  local copies, waits for them, and re-layouts: 39.5 us -> 65.3 us
  matrix products: 37.9 us -> 27.8 us
    all_gather x0 -> x4, waiting for transfers between devices: none -> 194 us  [from_root(): x = jnp.sum(lax.all_gather(x, axis), axis=0)]
    psum x4 -> x0, waiting for transfers between devices: 157 us -> none  [from_root(): x = lax.psum(x, axis)]
    reduce_sum x0 -> x4, other arithmetic: none -> 22.1 us  [from_root(): x = jnp.sum(lax.all_gather(x, axis), axis=0)]
    all_gather x2, waiting for transfers between devices: 0.02 us -> 19.6 us  [spread(): lax.all_gather(own, axis, axis=0, tiled=True)[:len(lines)].reshape(x.shape)]
    mul x3, local copies, waits for them, and re-layouts: 1.81 us -> 15.7 us  [apply_update(): product.reshape(row_count // TILE, TILE, width // TILE, TILE)]
    dot_general x3, matrix products: 18.6 us -> 7.27 us  [apply_update(): jnp.dot(shared, upper_rows[:, first_col:last_col], preferred_element_type...]
    unnamed x14 -> x23, local copies, waits for them, and re-layouts: 13.2 us -> 21.8 us
  transfers between devices with their start and end apart: 10 -> 10, of which waited for: 7 -> 9; matrix products, arithmetic and copies ran while one was open for 13% -> 16% of each run, Pallas kernels for 0% -> 0%
where the time goes in v1:
time: 551 us; the launch traced here: 546 us
  waiting for transfers between devices  259 us (47%)
  other arithmetic  110 us (20%)
  local copies, waits for them, and re-layouts  65.3 us (12%)
  blocking collectives  52.8 us (10%)
  matrix products  27.8 us (5%)
  between operations  15.5 us (3%)
  starting transfers between devices  14.9 us (3%)
    all_gather x4, waiting for transfers between devices, from_root(): x = jnp.sum(lax.all_gather(x, axis), axis=0)  194 us
    all_to_all x1, blocking collectives, cut_exchange(): lax.all_to_all(piece, axis, split_axis=0, concat_axis=0, tiled=True)  52.8 us
    scatter-add x1, other arithmetic, body(): matrix = front_in.reshape(tile_rows, TILE, tile_cols, TILE).at[local_row,...  46.9 us
    all_to_all x2, waiting for transfers between devices, cut_exchange(): lax.all_to_all(piece, axis, split_axis=0, concat_axis=0, tiled=True)  34.4 us
    reduce_sum x4, other arithmetic, from_root(): x = jnp.sum(lax.all_gather(x, axis), axis=0)  22.1 us
    unnamed x23, local copies, waits for them, and re-layouts  21.8 us
    dot_general x2, matrix products, factor_panel(): jnp.dot(matrix[:, first_col:first_col + PANEL], inverse[panel_index], pre...  20.5 us
    all_gather x2, waiting for transfers between devices, spread(): lax.all_gather(own, axis, axis=0, tiled=True)[:len(lines)].reshape(x.shape)  19.6 us
  transfers between devices with their start and end apart: 10, of which 9 were waited for; matrix products, arithmetic and copies ran while one was open for 16% of the time, Pallas kernels for 0%

profile of v1, /device:TPU:1, one launch (start us, length us, event | category | flops | bytes accessed | tf_op | source)
XLA Modules:
  0.0 546.3 jit_solution(2128556457595577470)
XLA Ops:
  9.9 9.6 %all-to-all-start = ((s32[32,1,7]{2,1,0:T(1,128)}), s32[32,1,7]{2,1,0:T(1,128)S(1)}, u32[]{:S(2)}, u32[]{:S(2)}) async-start(s32[32,1,7]{2,1,0:T(1,128)} %bitcast), calls=%async_computation | async-start | bytes 32768 | tf_op jit(solution)/shard_map/all_to_all | solution.py:49
  19.5 8.1 %fusion.22 = (bf16[32,1,7,64,128]{4,3,2,1,0:T(8,128)(2,1)}, bf16[32,1,7,64,128]{4,3,2,1,0:T(8,128)(2,1)}) fusion(bf16[32,1,7,128,128]{4,3,2,1,0:T(8,128)(2,1)} %bitcast.110), kind=kLoop, calls=%fused_computation.61 | loop fusion | bytes 14680064 | tf_op jit(solution)/shard_map/split | solution.py:47
  27.7 52.8 %all_to_all.15 = bf16[32,1,7,64,128]{4,3,2,1,0:T(8,128)(2,1)} all-to-all(bf16[32,1,7,64,128]{4,3,2,1,0:T(8,128)(2,1)} %get-tuple-element.73), channel_id=1, replica_groups=mesh['front'=4,'row'=4,'col_0'=4,'col_1'=2] {'row','col_0','col_1'}, dimensions={0} | all-to-all | bytes 7340032 | tf_op jit(solution)/shard_map/all_to_all | solution.py:49
  85.3 5.5 %copy.43 = f32[256,8,8,128]{3,2,1,0:T(8,128)S(1)} copy(f32[256,8,8,128]{3,1,2,0:T(8,128)} %bitcast.107) | data formatting | bytes 16777216
  90.8 4.9 copy.31
  96.5 34.4 %all-to-all-done.2 = bf16[32,1,7,64,128]{4,3,2,1,0:T(8,128)(2,1)} async-done(((bf16[32,1,7,64,128]{4,3,2,1,0:T(8,128)(2,1)}), bf16[32,1,7,64,128]{4,3,2,1,0:T(8,128)(2,1)}, u32[]{:S(2)}, u32[]{:S(2)}) %all-to-all-start.2) | async-done | bytes 3670048 | tf_op jit(solution)/shard_map/all_to_all | solution.py:49
  130.9 8.9 %pad_maximum_fusion = bf16[32,1,7,128,128]{4,3,2,1,0:T(8,128)(2,1)} fusion(bf16[32,1,7,64,128]{4,3,2,1,0:T(8,128)(2,1)} %all-to-all-done.2, bf16[32,1,7,64,128]{4,3,2,1,0:T(8,128)(2,1)} %all_to_all.15), kind=kLoop, calls=%fused_computation.5 | loop fusion | flops 14680064 | bytes 14680064 | tf_op jit(solution)/shard_map/concatenate | solution.py:50
  139.8 10.1 %bitcast_convert_fusion = f32[224,128,128]{2,1,0:T(8,128)} fusion(bf16[32,1,7,128,128]{4,3,2,1,0:T(8,128)(2,1)} %pad_maximum_fusion), kind=kLoop, calls=%fused_computation.6 | loop fusion | flops 3670016 | bytes 22020096 | tf_op jit(solution)/shard_map/convert_element_type | solution.py:115
  149.9 46.9 %scatter_fusion = f32[16,128,8,128]{3,1,2,0:T(8,128)} fusion(f32[16,128,8,128]{3,1,2,0:T(8,128)} %copy.31, s32[224]{0:T(256)S(1)} %bitcast.106, f32[224,128,128]{2,1,0:T(8,128)} %bitcast_convert_fusion), kind=kCustom, calls=%fused_computation | custom fusion | flops 3670016 | bytes 44041984 | tf_op jit(solution)/shard_map/scatter-add | solution.py:122
  200.7 9.9 %copy.32 = f32[16,128,8,128]{3,2,1,0:T(8,128)S(1)} copy(f32[16,128,8,128]{3,1,2,0:T(8,128)} %scatter_fusion) | data formatting | bytes 16777216 | tf_op jit(solution)/shard_map/scatter-add | solution.py:122
  212.8 8.6 %convert_select_fusion.1 = (bf16[2048,512]{1,0:T(8,128)(2,1)}, f32[2048,512]{1,0:T(8,128)}) fusion(pred[]{:T(512)S(6)} %eq.6, f32[2,512,512]{2,1,0:T(8,128)S(1)} %copy-done.3, f32[2048,1024]{1,0:T(8,128)S(1)} %bitcast.96), kind=kOutput, calls=%fused_computation.26 | convolution fusion | flops 6444548096 | bytes 11534337 | tf_op jit(solution)/shard_map/dot_general | solution.py:71
  223.2 81.8 %all-gather.15.cloned.1.call-done = bf16[8192,512]{1,0:T(8,128)(2,1)} async-done(((bf16[2048,512]{1,0:T(8,128)(2,1)}), bf16[8192,512]{1,0:T(8,128)(2,1)}) %all-gather.15.cloned.1.call-update) | async-done | bytes 8388624 | tf_op jit(solution)/shard_map/all_gather | solution.py:20
  305.0 6.7 %reduce_sum.48 = bf16[2048,512]{1,0:T(8,128)(2,1)} reduce(bf16[4,2048,512]{2,1,0:T(8,128)(2,1)} %bitcast.108, bf16[]{:T(256)} %constant.196.clone.1), dimensions={0}, to_apply=%region_2.3 | reduce | flops 3145728 | bytes 10485762 | tf_op jit(solution)/shard_map/reduce_sum | solution.py:20
  313.7 6.1 %fusion.2 = f32[2048,1024]{1,0:T(8,128)} fusion(f32[2048,1024]{1,0:T(8,128)} %bitcast.97, f32[2048,512]{1,0:T(8,128)} %get-tuple-element.82, pred[2048]{0:T(1024)(128)(4,1)S(1)} %broadcast_and_fusion.1, pred[]{:T(512)} %compare_reduce_fusion), kind=kLoop, calls=%fused_computation.9 | loop fusion | flops 2097152 | bytes 12585472 | tf_op jit(solution)/shard_map/scatter | solution.py:136
  319.8 8.3 %copy.63 = f32[2048,1024]{1,0:T(8,128)} copy(f32[2048,1024]{1,0:T(8,128)} %fusion.2) | data formatting | bytes 16777216
  331.4 18.9 %all-gather.17.cloned.1.call-done = bf16[4096,512]{1,0:T(8,128)(2,1)} async-done(((bf16[2048,512]{1,0:T(8,128)(2,1)}), bf16[4096,512]{1,0:T(8,128)(2,1)}) %all-gather.17.cloned.1.call-update) | async-done | bytes 4194320 | tf_op jit(solution)/shard_map/all_gather | solution.py:20
  372.1 11.9 %fusion.7 = (f32[2048,1024]{1,0:T(8,128)}, bf16[2048,512]{1,0:T(8,128)(2,1)S(1)}) fusion(f32[2048,1024]{1,0:T(8,128)} %copy-done, pred[2048]{0:T(1024)(128)(4,1)S(1)} %broadcast_and_fusion, f32[2,512,512]{2,1,0:T(8,128)S(1)} %copy-done.4, f32[256,8,4,128]{3,2,1,0:T(4,128)} %bitcast.99, f32[2048,1024]{1,0:T(8,128)} %fusion.2, ...), kind=kOutput, calls=%fused_computation.17 | convolution fusion | flops 6448742400 | bytes 19927552 | tf_op jit(solution)/shard_map/dot_general | solution.py:71
  385.5 9.8 %reduce-scatter.5.cloned.1.call-done = bf16[128,1024]{1,0:T(8,128)(2,1)} async-done(((bf16[512,1024]{1,0:T(8,128)(2,1)}), bf16[128,1024]{1,0:T(8,128)(2,1)}) %reduce-scatter.5.cloned.1.call-update) | async-done | bytes 262160 | tf_op jit(solution)/shard_map/reduce_scatter | solution.py:65
  395.3 74.2 %all-gather.19.cloned.1.call-done = bf16[8192,512]{1,0:T(8,128)(2,1)} async-done(((bf16[2048,512]{1,0:T(8,128)(2,1)}), bf16[8192,512]{1,0:T(8,128)(2,1)}) %all-gather.19.cloned.1.call-update) | async-done | bytes 8388624 | tf_op jit(solution)/shard_map/all_gather | solution.py:20
  469.5 6.6 %reduce_sum.50 = bf16[2048,512]{1,0:T(8,128)(2,1)} reduce(bf16[4,2048,512]{2,1,0:T(8,128)(2,1)} %bitcast.109, bf16[]{:T(256)} %constant.196.clone.1), dimensions={0}, to_apply=%region_5.6 | reduce | flops 3145728 | bytes 10485762 | tf_op jit(solution)/shard_map/reduce_sum | solution.py:20
  476.2 18.0 %all-gather.13.cloned.1.call-done = bf16[512,1024]{1,0:T(8,128)(2,1)} async-done(((bf16[128,1024]{1,0:T(8,128)(2,1)}), bf16[512,1024]{1,0:T(8,128)(2,1)}) %all-gather.13.cloned.1.call-update) | async-done | bytes 1048592 | tf_op jit(solution)/shard_map/all_gather | solution.py:66
  496.0 19.0 %all-gather.21.cloned.1.call-done = bf16[4096,512]{1,0:T(8,128)(2,1)} async-done(((bf16[2048,512]{1,0:T(8,128)(2,1)}), bf16[4096,512]{1,0:T(8,128)(2,1)}) %all-gather.21.cloned.1.call-update) | async-done | bytes 4194320 | tf_op jit(solution)/shard_map/all_gather | solution.py:20
  519.4 4.7 broadcast_multiply_fusion
  524.1 10.1 %copy.39 = f32[16,128,8,128]{3,2,1,0:T(8,128)S(1)} copy(f32[16,128,8,128]{3,1,2,0:T(8,128)} %broadcast_multiply_fusion) | data formatting | bytes 16777216 | tf_op jit(solution)/shard_map/mul | solution.py:91
  (75 shorter events, 55.0 us)
Async XLA Ops:
  9.9 17.7 %all-to-all-start = ((s32[32,1,7]{2,1,0:T(1,128)}), s32[32,1,7]{2,1,0:T(1,128)S(1)}, u32[]{:S(2)}, u32[]{:S(2)}) async-start(s32[32,1,7]{2,1,0:T(1,128)} %bitcast), calls=%async_computation | async-start | bytes 32768 | tf_op jit(solution)/shard_map/all_to_all | solution.py:49
  80.5 50.4 %all-to-all-start.2 = ((bf16[32,1,7,64,128]{4,3,2,1,0:T(8,128)(2,1)}), bf16[32,1,7,64,128]{4,3,2,1,0:T(8,128)(2,1)}, u32[]{:S(2)}, u32[]{:S(2)}) async-start(bf16[32,1,7,64,128]{4,3,2,1,0:T(8,128)(2,1)} %get-tuple-element.74), calls=%async_computation.2 | async-start | bytes 7340032 | tf_op jit(solution)/shard_map/all_to_all | solution.py:49
  85.1 138.1 %reduce-scatter.3.cloned.1.call-start = ((), (), s32[]{:S(2)}) async-start(), calls=%async_computation.5 | async-start | bytes 1310720 | tf_op jit(solution)/shard_map/reduce_scatter | solution.py:65
  200.5 104.5 %all-gather.15.cloned.1.call-start = ((), (), s32[]{:S(2)}) async-start(), calls=%async_computation.9 | async-start | bytes 10485760 | tf_op jit(solution)/shard_map/all_gather | solution.py:20
  210.7 2.2 copy-start.3
  212.8 8.6 %copy-start.1 = (f32[256,8,8,128]{3,1,2,0:T(8,128)}, f32[256,8,8,128]{3,1,2,0:T(8,128)S(1)}, u32[]{:S(2)}) copy-start(f32[256,8,8,128]{3,1,2,0:T(8,128)S(1)} %copy.59) | copy-start | bytes 25165828
  221.4 108.2 %all-gather.11.cloned.1.call-start = ((), (), s32[]{:S(2)}) async-start(), calls=%async_computation.6 | async-start | bytes 1310720 | tf_op jit(solution)/shard_map/all_gather | solution.py:66
  223.2 127.1 %all-gather.17.cloned.1.call-start = ((), (), s32[]{:S(2)}) async-start(), calls=%async_computation.10 | async-start | bytes 6291456 | tf_op jit(solution)/shard_map/all_gather | solution.py:20
  311.7 83.6 %reduce-scatter.5.cloned.1.call-start = ((), (), s32[]{:S(2)}) async-start(), calls=%async_computation.7 | async-start | bytes 1310720 | tf_op jit(solution)/shard_map/reduce_scatter | solution.py:65
  358.8 4.1 copy-start.2
  358.8 4.1 slice-start
  360.1 3.7 slice-start.1
  365.4 6.7 %copy-start.4 = (f32[2,512,512]{2,1,0:T(8,128)S(1)}, f32[2,512,512]{2,1,0:T(8,128)}, u32[]{:S(2)}) copy-start(f32[2,512,512]{2,1,0:T(8,128)} %param.21) | copy-start | bytes 6291460
  367.6 3.2 copy-start
  372.0 97.6 %all-gather.19.cloned.1.call-start = ((), (), s32[]{:S(2)}) async-start(), calls=%async_computation.11 | async-start | bytes 10485760 | tf_op jit(solution)/shard_map/all_gather | solution.py:20
  385.4 108.8 %all-gather.13.cloned.1.call-start = ((), (), s32[]{:S(2)}) async-start(), calls=%async_computation.8 | async-start | bytes 1310720 | tf_op jit(solution)/shard_map/all_gather | solution.py:66
  395.3 119.7 %all-gather.21.cloned.1.call-start = ((), (), s32[]{:S(2)}) async-start(), calls=%async_computation.12 | async-start | bytes 6291456 | tf_op jit(solution)/shard_map/all_gather | solution.py:20
  519.4 14.8 %slice-start.2 = ((s8[8388608]{0:T(1024)(128)(4,1)}), s8[4194304]{0:T(1024)(128)(4,1)S(1)}, s32[]{:S(2)}) async-start(s8[8388608]{0:T(1024)(128)(4,1)} %bitcast.94), calls=%async_computation.15 | async-start | bytes 8388608
  524.1 10.1 %slice-start.3 = ((s8[8388608]{0:T(1024)(128)(4,1)}), s8[4194304]{0:T(1024)(128)(4,1)S(1)}, s32[]{:S(2)}) async-start(s8[8388608]{0:T(1024)(128)(4,1)} %bitcast.94), calls=%async_computation.16 | async-start | bytes 8388608
Sparse Core Ops, SparseCore 0:
  200.6 22.5 reduce-scatter.2
  372.1 23.0 reduce-scatter.4
Sparse Core Ops, SparseCore 1:
  221.5 83.4 all-gather.14
  306.6 23.0 all-gather.10
  331.3 19.0 all-gather.16
  385.5 84.0 all-gather.18
  471.2 23.0 all-gather.12
  495.9 19.0 all-gather.20
